TPU v7x, 128 devices: a whole 4x4x4 slice. The times are simulated.
128 devices in a mesh: dp: 16 (over y_hi, z, core), cache: 8 (over y_lo, x).
Axes of the slice: x: 4, y: 4 (y_hi: 2, y_lo: 2; y = y_hi * 2 + y_lo), z: 4, core: 2. Of those that a mesh axis runs over, the one named last changes fastest.
Arguments:
- hidden_in: bfloat16 [16384, 2560], P(('dp', 'cache')), may hold values from -6 to 6
- placing: int32 [16384], P('dp'), may hold values from 0 to 16383, as said below
- prompt_start: int32 [16384], P(('dp', 'cache')), may hold values from 0 to 16383, as said below
- attn_gain: float32 [2560], replicated, may hold values from 0.5 to 1.5
- w_qkv: bfloat16 [2560, 1792], P(('dp', 'cache'))
- w_out: bfloat16 [1280, 2560], P(('dp', 'cache')), may hold values from -0.15625 to 0.15625
- moe_gain: float32 [2560], replicated, may hold values from 0.5 to 1.5
- routes: int32 [16384, 6], P(('dp', 'cache')), may hold values from 0 to 63, all different within a row; in each aligned block of 128 rows (0 to 127, 128 to 255, ...) at most 16 rows name the same one
- route_weight: float32 [16384, 6], P(('dp', 'cache')), may hold values from 0.05 to 0.35
- w_gate_up: bfloat16 [128, 2560, 1536], P(('dp', 'cache')), may hold values from -0.125 to 0.125
- w_down: bfloat16 [128, 768, 2560], P(('dp', 'cache')), may hold values from -0.15625 to 0.15625
Outputs:
- mixed: bfloat16 [16384, 2560], P(('dp', 'cache'))
- cache_keys: bfloat16 [16384, 256], P(('dp', 'cache'))
- cache_values: bfloat16 [16384, 256], P(('dp', 'cache'))
Inputs may be any that keep to these rules, and one draw needn't show every extreme that they name: `placing`: a permutation of the 16384 positions; dealt rows g * 1024 to (g+1) * 1024 - 1 hold natural positions of the same range, and the dealt rows c * 128 + j * 16 to c * 128 + (j+1) * 16 - 1 of a group hold natural positions of its span j * 128 to (j+1) * 128 - 1. Prompts are runs of consecutive natural positions inside one group of 1024, of at most 512 tokens, some of exactly 512; prompt_start[r] <= placing[r] and it is the first position of that run. `routes`: in the rows of one device (aligned blocks of 128 rows) no expert is named more than 16 times.
All inputs are finite; a program needn't handle non-finite values.
Results may differ from a plain program's by a relative error of at most 0.014.
Values may be sent and summed in bfloat16 or wider, within the bound.
No kernel may reach another device: no remote copies, remote signals or barrier semaphores. Data moves between devices by JAX's collectives and lax.ppermute only.
A program may use at most 128 MiB of HBM per device.

v0:
```python
import jax
import jax.numpy as jnp
from jax import lax
from jax.sharding import PartitionSpec as P

HD = 128
QH = 10
KVH = 2
TOP = 6


norm_eps = 1e-05
rope_base = 500000.0
masked_score = -1e30


def rms_scaled(features, gain_vector):
    widened = features.astype(jnp.float32)
    factor = lax.rsqrt(jnp.mean(widened * widened, axis=-1, keepdims=True) + norm_eps)
    return (widened * factor * gain_vector).astype(jnp.bfloat16)


def rotated(projected, position, head_count):
    row_count = projected.shape[0]
    grouped = projected.reshape(row_count, head_count, HD)
    half_size = HD // 2
    inverse = rope_base ** (-(jnp.arange(half_size, dtype=jnp.float32) * 2.0 / HD))
    angles = position.astype(jnp.float32)[:, None] * inverse[None, :]
    cosine = jnp.cos(angles)[:, None, :]
    sine_part = jnp.sin(angles)[:, None, :]
    first_half = grouped[..., :half_size]
    second = grouped[..., half_size:]
    turned = jnp.concatenate(
        [first_half * cosine - second * sine_part, second * cosine + first_half * sine_part],
        axis=-1,
    )
    return turned.reshape(row_count, head_count * HD).astype(jnp.bfloat16)


def expert_half(slot_block, gate_up, down_part):
    flat_rows = slot_block.reshape(-1, slot_block.shape[-1])
    joined = jnp.dot(flat_rows, gate_up, preferred_element_type=jnp.float32)
    half_size = gate_up.shape[1] // 2
    active = (jax.nn.silu(joined[:, :half_size]) * joined[:, half_size:]).astype(jnp.bfloat16)
    return (
        jnp.dot(active, down_part, preferred_element_type=jnp.float32)
        .astype(jnp.bfloat16)
        .reshape(slot_block.shape)
    )


def per_device(
    hidden_in,
    placing,
    prompt_start,
    attn_gain,
    w_qkv,
    w_out,
    moe_gain,
    routes,
    route_weight,
    w_gate_up,
    w_down,
):
    row_count = hidden_in.shape[0]
    model_width = hidden_in.shape[1]
    cache_size = lax.axis_size("cache")
    my_index = lax.axis_index("cache")
    deal_rows = row_count // cache_size
    query_width = QH * HD
    kv_width = KVH * HD
    group_base = lax.axis_index("dp") * placing.shape[0]
    my_place = lax.dynamic_slice_in_dim(placing, my_index * row_count, row_count)
    position = my_place - prompt_start
    normed = rms_scaled(hidden_in, attn_gain)
    full_qkv, full_out = (
        lax.all_gather(w_qkv, ("dp", "cache"), axis=0, tiled=True),
        lax.all_gather(w_out, ("dp", "cache"), axis=0, tiled=True),
    )
    projected = jnp.dot(normed, full_qkv, preferred_element_type=jnp.float32)
    queries = rotated(projected[:, :query_width], position, QH)
    keys_here = rotated(projected[:, query_width : query_width + kv_width], position, KVH)
    values_here = projected[:, query_width + kv_width :].astype(jnp.bfloat16)
    group_size = QH // KVH
    query_heads = queries.reshape(row_count, KVH, group_size, HD)
    score_scale = HD ** (-0.5)
    highest = jnp.full((row_count, KVH, group_size), masked_score, jnp.float32)
    key_piece = lax.all_gather(keys_here, "cache", axis=0, tiled=True)
    value_piece = lax.all_gather(values_here, "cache", axis=0, tiled=True)
    piece_rows = key_piece.shape[0]
    key_heads = key_piece.reshape(piece_rows, KVH, HD)
    value_heads = value_piece.reshape(piece_rows, KVH, HD)
    scores = (
        jnp.einsum("tkgd,rkd->tkgr", query_heads, key_heads, preferred_element_type=jnp.float32)
        * score_scale
    )
    allowed = (placing[None, :] >= prompt_start[:, None]) & (placing[None, :] <= my_place[:, None])
    allowed = allowed[:, None, None, :]
    new_highest = jnp.maximum(highest, jnp.max(jnp.where(allowed, scores, masked_score), axis=-1))
    weights = jnp.where(allowed, jnp.exp(scores - new_highest[..., None]), 0.0)
    denominator = jnp.sum(weights, axis=-1)
    numerator = jnp.einsum(
        "tkgr,rkd->tkgd",
        weights.astype(jnp.bfloat16),
        value_heads,
        preferred_element_type=jnp.float32,
    )
    highest, denominator, numerator = (new_highest, denominator, numerator)
    context = (
        (numerator / denominator[..., None]).reshape(row_count, query_width).astype(jnp.bfloat16)
    )
    attn_out = jnp.dot(context, full_out, preferred_element_type=jnp.float32)
    attended = (hidden_in.astype(jnp.float32) + attn_out).astype(jnp.bfloat16)
    moe_in = rms_scaled(attended, moe_gain)
    device_count = lax.axis_size(("dp", "cache"))
    expert_count = device_count // 2
    capacity = 4 * row_count * TOP // (3 * expert_count)
    expert_ids = routes.reshape(-1)
    one_hot = (expert_ids[:, None] == jnp.arange(expert_count, dtype=jnp.int32)[None, :]).astype(
        jnp.int32
    )
    slot_rank = jnp.sum((jnp.cumsum(one_hot, axis=0) - one_hot) * one_hot, axis=1)
    slot_index = expert_ids * capacity + slot_rank
    source_row = (
        jnp.full((expert_count * capacity,), row_count, jnp.int32)
        .at[slot_index]
        .set(jnp.arange(row_count * TOP, dtype=jnp.int32) // TOP)
    )
    padded = jnp.concatenate([moe_in, jnp.zeros((1, model_width), jnp.bfloat16)], axis=0)
    outgoing = padded[source_row].reshape(expert_count, capacity, model_width)
    partial_value = expert_half(
        lax.all_to_all(
            jnp.repeat(outgoing, 2, axis=0),
            ("dp", "cache"),
            split_axis=0,
            concat_axis=0,
            tiled=True,
        ),
        w_gate_up[0],
        w_down[0],
    )
    returned = lax.all_to_all(
        partial_value, ("dp", "cache"), split_axis=0, concat_axis=0, tiled=True
    )
    halves = returned.reshape(expert_count, 2, capacity, model_width).astype(jnp.float32)
    merged = (halves[:, 0] + halves[:, 1]).astype(jnp.bfloat16)
    picked = merged.reshape(expert_count * capacity, model_width)[slot_index].reshape(
        row_count, TOP, model_width
    )
    mixture = jnp.sum(route_weight[:, :, None] * picked.astype(jnp.float32), axis=1)
    finished = (attended.astype(jnp.float32) + mixture).astype(jnp.bfloat16)
    package = (
        finished.reshape(cache_size, deal_rows, model_width),
        keys_here.reshape(cache_size, deal_rows, kv_width),
        values_here.reshape(cache_size, deal_rows, kv_width),
    )
    home_rows, home_keys, home_values = (
        lax.all_to_all(package[0], "cache", split_axis=0, concat_axis=0, tiled=True),
        lax.all_to_all(package[1], "cache", split_axis=0, concat_axis=0, tiled=True),
        lax.all_to_all(package[2], "cache", split_axis=0, concat_axis=0, tiled=True),
    )
    sender_rows = (
        jnp.arange(cache_size, dtype=jnp.int32)[:, None] * row_count
        + my_index * deal_rows
        + jnp.arange(deal_rows, dtype=jnp.int32)[None, :]
    ).reshape(-1)
    target = placing[sender_rows] - group_base - my_index * row_count
    mixed = (
        jnp.zeros((row_count, model_width), jnp.bfloat16)
        .at[target]
        .set(home_rows.reshape(-1, model_width))
    )
    cache_keys = (
        jnp.zeros((row_count, kv_width), jnp.bfloat16)
        .at[target]
        .set(home_keys.reshape(-1, kv_width))
    )
    cache_values = (
        jnp.zeros((row_count, kv_width), jnp.bfloat16)
        .at[target]
        .set(home_values.reshape(-1, kv_width))
    )
    return (mixed, cache_keys, cache_values)


def solution(mesh):
    in_specs = (
        P(("dp", "cache"), None),
        P("dp"),
        P(("dp", "cache")),
        P(),
        P(("dp", "cache"), None),
        P(("dp", "cache"), None),
        P(),
        P(("dp", "cache"), None),
        P(("dp", "cache"), None),
        P(("dp", "cache"), None, None),
        P(("dp", "cache"), None, None),
    )
    out_specs = (P(("dp", "cache"), None), P(("dp", "cache"), None), P(("dp", "cache"), None))
    return jax.shard_map(
        per_device, mesh=mesh, in_specs=in_specs, out_specs=out_specs, check_vma=False
    )
```

profile of v0, /device:TPU:1, one launch (start us, length us, event | category | flops | bytes accessed | tf_op | source)
XLA Modules:
  0.0 1167.8 jit_solution(6544326137829235413)
XLA Ops:
  19.8 312.4 %all-gather.7.cloned.1.call-done = bf16[128,10,2560]{2,1,0:T(8,128)(2,1)} async-done(((bf16[1,10,2560]{2,1,0:T(8,128)(2,1)}), bf16[128,10,2560]{2,1,0:T(8,128)(2,1)}) %all-gather.7.cloned.1.call-update) | async-done | bytes 6553616 | tf_op jit(solution)/shard_map/all_gather | solution.py:78
  332.2 12.8 %reshape.368 = bf16[1280,2560]{1,0:T(8,128)(2,1)} reshape(bf16[128,10,2560]{2,1,0:T(8,128)(2,1)} %all-gather.7.cloned.1.call-done) | data formatting | bytes 13107200
  345.0 308.4 %all-gather.5.cloned.1.call-done = bf16[128,20,1792]{2,1,0:T(8,128)(2,1)} async-done(((bf16[1,20,1792]{2,1,0:T(8,128)(2,1)}), bf16[128,20,1792]{2,1,0:T(8,128)(2,1)}) %all-gather.5.cloned.1.call-update) | async-done | bytes 9175056 | tf_op jit(solution)/shard_map/all_gather | solution.py:77
  653.3 13.2 %reshape.366 = bf16[2560,1792]{1,0:T(8,128)(2,1)} reshape(bf16[128,20,1792]{2,1,0:T(8,128)(2,1)} %all-gather.5.cloned.1.call-done) | data formatting | bytes 18350080
  666.5 5.0 fusion.30
  672.2 23.9 %all_gather.13 = bf16[1024,256]{1,0:T(8,128)(2,1)S(1)} all-gather(bf16[128,256]{1,0:T(8,128)(2,1)} %slice.95), channel_id=1, replica_groups=mesh['dp'=16,'cache'=8] {'cache'}, dimensions={0}, use_global_device_ids=true | all-gather | bytes 589824 | tf_op jit(solution)/shard_map/all_gather | solution.py:89
  697.0 21.0 %all_gather.14 = bf16[1024,256]{0,1:T(8,128)(2,1)S(1)} all-gather(bf16[128,256]{0,1:T(8,128)(2,1)S(1)} %bitcast.117), channel_id=1, replica_groups=mesh['dp'=16,'cache'=8] {'cache'}, dimensions={0}, use_global_device_ids=true | all-gather | bytes 589824 | tf_op jit(solution)/shard_map/all_gather | solution.py:88
  724.3 6.3 gather_fusion.1
  730.6 7.8 broadcast_in_dim.35
  738.4 137.9 %all_to_all.25 = bf16[128,16,2560]{2,1,0:T(8,128)(2,1)S(1)} all-to-all(bf16[128,16,2560]{2,1,0:T(8,128)(2,1)} %bitcast.107), channel_id=1, replica_groups=mesh['dp'=16,'cache'=8] {'dp','cache'}, dimensions={0} | all-to-all | bytes 20971520 | tf_op jit(solution)/shard_map/all_to_all | solution.py:132
  876.3 21.6 %fusion.2 = f32[2048,1536]{1,0:T(8,128)} fusion(bf16[2048,2560]{1,0:T(8,128)(2,1)S(1)} %bitcast.110, bf16[1,2560,1536]{2,1,0:T(8,128)(2,1)} %param.20), kind=kOutput, calls=%fused_computation.13 | convolution fusion | flops 16106127360 | bytes 30932992 | tf_op jit(solution)/shard_map/dot_general | solution.py:42
  897.9 17.3 %convolution_convert_fusion = bf16[2048,2560]{1,0:T(8,128)(2,1)} fusion(bf16[1,768,2560]{2,1,0:T(8,128)(2,1)S(1)} %copy-done.5, f32[2048,1536]{1,0:T(8,128)} %fusion.2), kind=kOutput, calls=%fused_computation.7 | convolution fusion | flops 8067743744 | bytes 27000832 | tf_op jit(solution)/shard_map/dot_general | solution.py:46
  915.2 10.0 all-to-all-start.1
  926.1 143.9 %all-to-all-done.1 = bf16[128,16,2560]{2,1,0:T(8,128)(2,1)} async-done(((bf16[128,16,2560]{2,1,0:T(8,128)(2,1)}), bf16[128,16,2560]{2,1,0:T(8,128)(2,1)}, u32[]{:S(2)}, u32[]{:S(2)}) %all-to-all-start.1) | async-done | bytes 10485792 | tf_op jit(solution)/shard_map/all_to_all | solution.py:142
  1069.9 13.3 %all-to-all-start.3 = ((bf16[8,16,256]{2,1,0:T(8,128)(2,1)}), bf16[8,16,256]{2,1,0:T(8,128)(2,1)S(1)}, u32[]{:S(2)}, u32[]{:S(2)}) async-start(bf16[8,16,256]{2,1,0:T(8,128)(2,1)} %convert_element_type.104), calls=%async_computation.3 | async-start | bytes 131072 | tf_op jit(solution)/shard_map/all_to_all | solution.py:159
  1083.3 14.1 %convert.14 = f32[64,2,16,2560]{3,2,1,0:T(8,128)} convert(bf16[64,2,16,2560]{3,2,1,0:T(8,128)(2,1)} %bitcast.24) | non-fusion elementwise | flops 5242880 | bytes 31457280 | tf_op jit(solution)/shard_map/convert_element_type | solution.py:145
  1097.3 11.1 fusion.1
  1108.4 11.5 gather_fusion.2
  1120.0 7.8 reshape.307
  1127.7 8.0 multiply_reduce_fusion
  1135.8 5.2 all-to-all-start.4
  1141.9 4.2 all-to-all-done.4
  1146.1 3.5 all-to-all-start.2
  1154.1 4.5 all-to-all-done.2
  (78 shorter events, 28.7 us)
Async XLA Ops:
  7.2 325.0 %all-gather.7.cloned.1.call-start = ((), (), s32[]{:S(2)}) async-start(), calls=%async_computation.6 | async-start | bytes 10567680 | tf_op jit(solution)/shard_map/all_gather | solution.py:78
  7.9 645.4 %all-gather.5.cloned.1.call-start = ((), (), s32[]{:S(2)}) async-start(), calls=%async_computation.5 | async-start | bytes 11096064 | tf_op jit(solution)/shard_map/all_gather | solution.py:77
  345.0 321.6 %copy-start.1 = (bf16[128,2560]{1,0:T(8,128)(2,1)S(1)}, bf16[128,2560]{1,0:T(8,128)(2,1)}, u32[]{:S(2)}) copy-start(bf16[128,2560]{1,0:T(8,128)(2,1)} %param.11) | copy-start | bytes 1966084
  345.0 321.6 %copy-start.2 = (f32[2560]{0:T(1024)S(1)}, f32[2560]{0:T(1024)}, u32[]{:S(2)}) copy-start(f32[2560]{0:T(1024)} %param.14) | copy-start | bytes 30724
  719.5 2.3 slice-start
  720.5 2.3 slice-start.1
  722.9 1.1 copy-start.3
  876.3 21.6 %copy-start.5 = (bf16[1,768,2560]{2,1,0:T(8,128)(2,1)S(1)}, bf16[1,768,2560]{2,1,0:T(8,128)(2,1)}, u32[]{:S(2)}) copy-start(bf16[1,768,2560]{2,1,0:T(8,128)(2,1)} %param.21) | copy-start | bytes 11796484
  915.2 10.0 copy-start.4
  915.2 154.7 %all-to-all-start.1 = ((bf16[128,16,2560]{2,1,0:T(8,128)(2,1)}), bf16[128,16,2560]{2,1,0:T(8,128)(2,1)}, u32[]{:S(2)}, u32[]{:S(2)}) async-start(bf16[128,16,2560]{2,1,0:T(8,128)(2,1)} %bitcast.109), calls=%async_computation.1 | async-start | bytes 20971520 | tf_op jit(solution)/shard_map/all_to_all | solution.py:142
  1069.9 65.8 %all-to-all-start.3 = ((bf16[8,16,256]{2,1,0:T(8,128)(2,1)}), bf16[8,16,256]{2,1,0:T(8,128)(2,1)S(1)}, u32[]{:S(2)}, u32[]{:S(2)}) async-start(bf16[8,16,256]{2,1,0:T(8,128)(2,1)} %convert_element_type.104), calls=%async_computation.3 | async-start | bytes 131072 | tf_op jit(solution)/shard_map/all_to_all | solution.py:159
  1127.7 22.1 %copy-start = (s32[1024]{0:T(1024)S(1)}, s32[1024]{0:T(1024)}, u32[]{:S(2)}) copy-start(s32[1024]{0:T(1024)} %param.12) | copy-start | bytes 12292
  1135.8 10.4 all-to-all-start.4
  1146.1 12.5 %all-to-all-start.2 = ((bf16[8,16,2560]{2,1,0:T(8,128)(2,1)}), bf16[8,16,2560]{2,1,0:T(8,128)(2,1)S(1)}, u32[]{:S(2)}, u32[]{:S(2)}) async-start(bf16[8,16,2560]{2,1,0:T(8,128)(2,1)} %bitcast.26), calls=%async_computation.2 | async-start | bytes 1310720 | tf_op jit(solution)/shard_map/all_to_all | solution.py:158
Sparse Core Ops, SparseCore 0:
  9.7 322.4 all-gather.6
  333.9 319.4 all-gather.4
where the time goes:
time: 1180 us; the launch traced here: 1170 us
  waiting for transfers between devices  775 us (66%)
  blocking collectives  183 us (16%)
  local copies, waits for them, and re-layouts  74.5 us (6%)
  matrix products  47.2 us (4%)
  other arithmetic  42 us (4%)
  starting transfers between devices  32.1 us (3%)
  between operations  14.4 us (1%)
    all_gather x1, waiting for transfers between devices, per_device(): lax.all_gather(w_out, ('dp', 'cache'), axis=0, tiled=True)  312 us
    all_gather x1, waiting for transfers between devices, per_device(): lax.all_gather(w_qkv, ('dp', 'cache'), axis=0, tiled=True)  308 us
    all_to_all x1, waiting for transfers between devices, per_device(): lax.all_to_all(partial_value, ('dp', 'cache'), split_axis=0, concat_axis=...  144 us
    all_to_all x1, blocking collectives, per_device(): lax.all_to_all(jnp.repeat(outgoing, 2, axis=0), ('dp', 'cache'), split_ax...  138 us
    unnamed x20, local copies, waits for them, and re-layouts  28 us
    all_gather x1, blocking collectives, per_device(): value_piece = lax.all_gather(values_here, 'cache', axis=0, tiled=True)  23.9 us
  transfers between devices with their start and end apart: 6, of which 5 were waited for; matrix products, arithmetic and copies ran while one was open for 7% of the time, Pallas kernels for 0%

commit v1 on v0

v1 whole, which is shorter than its diff:
```python
import jax
import jax.numpy as jnp
import numpy as np
from jax import lax
from jax.sharding import Mesh
from jax.sharding import PartitionSpec as P

HD = 128
QH = 10
KVH = 2
TOP = 6
MOST = 16

DP = ("yh", "z", "core")
CACHE = ("yl", "x")
SIZES = {"yh": 2, "z": 4, "core": 2, "yl": 2, "x": 4}
ALL = DP + CACHE
CHIPS = ("yh", "z", "yl", "x")
CHIP_COUNT = 64

norm_eps = 1e-05
rope_base = 500000.0
masked_score = -1e30


def linear(yh, z, core, yl, x):
    return (((yh * 4 + z) * 2 + core) * 2 + yl) * 4 + x


def swap_pairs():
    pairs = []
    for yh in range(2):
        for z in range(4):
            for yl in range(2):
                for x in range(0, 4, 2):
                    low = linear(yh, z, 1, yl, x)
                    high = linear(yh, z, 0, yl, x + 1)
                    pairs += [(low, high), (high, low)]
    return pairs


def rms_scaled(features, gain_vector):
    widened = features.astype(jnp.float32)
    factor = lax.rsqrt(jnp.mean(widened * widened, axis=-1, keepdims=True) + norm_eps)
    return (widened * factor * gain_vector).astype(jnp.bfloat16)


def rotated(grouped, cosine, sine_part):
    half_size = HD // 2
    first_half = grouped[..., :half_size]
    second = grouped[..., half_size:]
    return jnp.concatenate(
        [first_half * cosine - second * sine_part, second * cosine + first_half * sine_part],
        axis=-1,
    ).astype(jnp.bfloat16)


def spread(shard, axes, count):
    return lax.all_to_all(
        jnp.broadcast_to(shard[None], (count,) + shard.shape), axes, 0, 0, tiled=True
    )


def expert_half(rows, gate_up, down_part):
    joined = jnp.dot(rows, gate_up, preferred_element_type=jnp.float32)
    half_size = gate_up.shape[1] // 2
    active = (jax.nn.silu(joined[:, :half_size]) * joined[:, half_size:]).astype(jnp.bfloat16)
    return jnp.dot(active, down_part, preferred_element_type=jnp.float32).astype(jnp.bfloat16)


def per_device(
    hidden_in,
    placing,
    prompt_start,
    attn_gain,
    w_qkv,
    w_out,
    moe_gain,
    routes,
    route_weight,
    w_gate_up,
    w_down,
):
    row_count, model_width = hidden_in.shape
    query_width = QH * HD
    kv_width = KVH * HD
    my_index = lax.axis_index(CACHE)
    group_rows = placing.shape[0]
    cache_size = group_rows // row_count
    deal_rows = row_count // cache_size
    group_base = lax.axis_index(DP) * group_rows

    pairs = swap_pairs()
    other_up = lax.ppermute(w_gate_up[0], ALL, pairs)
    other_down = lax.ppermute(w_down[0], ALL, pairs)
    keep = lax.axis_index("x") % 2 == lax.axis_index("core")

    qkv_rows = spread(w_qkv, CACHE, cache_size).reshape(-1, w_qkv.shape[1])
    full_qkv = lax.all_gather(qkv_rows, DP, axis=0, tiled=True)
    out_rows = spread(w_out, CACHE, cache_size).reshape(-1, w_out.shape[1])
    full_out = lax.all_gather(out_rows, DP, axis=0, tiled=True)
    full_qkv, other_up = lax.optimization_barrier((full_qkv, other_up))
    full_out, other_down = lax.optimization_barrier((full_out, other_down))

    my_place = lax.dynamic_slice_in_dim(placing, my_index * row_count, row_count)
    position = my_place - prompt_start

    bits = routes
    chip_of = (
        (bits & 0b111000)
        | ((bits & 0b000011) << 1)
        | ((bits & 0b000100) >> 2)
    )
    named = chip_of[:, :, None] == jnp.arange(CHIP_COUNT, dtype=jnp.int32)[None, None, :]
    member = jnp.any(named, axis=1)
    weight_of = jnp.sum(jnp.where(named, route_weight[:, :, None], 0.0), axis=1)
    row_ids = jnp.arange(row_count, dtype=jnp.int32)
    before = (row_ids[:, None] > row_ids[None, :]).astype(jnp.bfloat16)
    rank = jnp.dot(before, member.astype(jnp.bfloat16), preferred_element_type=jnp.float32)
    rank = jnp.where(member, rank.astype(jnp.int32), -1).T
    chosen = rank[:, None, :] == jnp.arange(MOST, dtype=jnp.int32)[None, :, None]
    chosen = chosen.reshape(CHIP_COUNT * MOST, row_count)
    pick = chosen.astype(jnp.bfloat16)
    weighted = jnp.where(
        chosen.reshape(CHIP_COUNT, MOST, row_count), weight_of.T[:, None, :], 0.0
    ).reshape(CHIP_COUNT * MOST, row_count)
    weighted_hi = lax.reduce_precision(weighted, 8, 7)
    weighted_lo = (weighted - weighted_hi).astype(jnp.bfloat16)
    blend = jnp.concatenate([weighted_hi.astype(jnp.bfloat16), weighted_lo], axis=1)

    normed = rms_scaled(hidden_in, attn_gain)
    projected = jnp.dot(normed, full_qkv, preferred_element_type=jnp.float32)
    half_size = HD // 2
    inverse = rope_base ** (-(jnp.arange(half_size, dtype=jnp.float32) * 2.0 / HD))
    angles = position.astype(jnp.float32)[:, None] * inverse[None, :]
    cosine = jnp.cos(angles)
    sine_part = jnp.sin(angles)
    keys_here = [
        rotated(projected[:, query_width + k * HD : query_width + (k + 1) * HD], cosine, sine_part)
        for k in range(KVH)
    ]
    values_here = projected[:, query_width + kv_width :].astype(jnp.bfloat16)
    kv_here = jnp.concatenate(keys_here + [values_here], axis=1)
    kv_group = spread(kv_here, CACHE, cache_size).reshape(group_rows, 2 * kv_width)
    queries = jnp.stack(
        [rotated(projected[:, h * HD : (h + 1) * HD], cosine, sine_part) for h in range(QH)]
    )
    allowed = (placing[None, :] >= prompt_start[:, None]) & (placing[None, :] <= my_place[:, None])
    contexts = []
    share = QH // KVH
    for k in range(KVH):
        key_head = kv_group[:, k * HD : (k + 1) * HD]
        value_head = kv_group[:, kv_width + k * HD : kv_width + (k + 1) * HD]
        scores = jnp.einsum(
            "htd,rd->htr",
            queries[k * share : (k + 1) * share],
            key_head,
            preferred_element_type=jnp.float32,
        ) * (HD ** (-0.5))
        scores = jnp.where(allowed[None], scores, masked_score)
        highest = jnp.max(scores, axis=-1, keepdims=True)
        weights = jnp.where(allowed[None], jnp.exp(scores - highest), 0.0)
        denominator = jnp.sum(weights, axis=-1, keepdims=True)
        numerator = jnp.einsum(
            "htr,rd->htd",
            weights.astype(jnp.bfloat16),
            value_head,
            preferred_element_type=jnp.float32,
        )
        contexts.append((numerator / denominator).astype(jnp.bfloat16))
    context = jnp.concatenate(contexts, axis=0)
    context = jnp.concatenate([context[h] for h in range(QH)], axis=1)
    attn_out = jnp.dot(context, full_out, preferred_element_type=jnp.float32)
    attended = (hidden_in.astype(jnp.float32) + attn_out).astype(jnp.bfloat16)
    moe_in = rms_scaled(attended, moe_gain)

    outgoing = jnp.dot(pick, moe_in, preferred_element_type=jnp.float32).astype(jnp.bfloat16)
    mine = lax.all_to_all(
        outgoing.reshape(CHIP_COUNT, MOST, model_width), CHIPS, 0, 0, tiled=True
    ).reshape(CHIP_COUNT * MOST, model_width)
    cores = [(0, 1), (1, 0)]
    mates = lax.ppermute(mine, "core", cores)
    gate_up = jnp.where(keep, w_gate_up[0], other_up)
    down_part = jnp.where(keep, w_down[0], other_down)
    for_mate = expert_half(mates, gate_up, down_part)
    from_mate = lax.ppermute(for_mate, "core", cores)
    own_part = expert_half(mine, gate_up, down_part)
    expert_out = (own_part.astype(jnp.float32) + from_mate.astype(jnp.float32)).astype(jnp.bfloat16)
    returned = lax.all_to_all(
        expert_out.reshape(CHIP_COUNT, MOST, model_width), CHIPS, 0, 0, tiled=True
    ).reshape(CHIP_COUNT * MOST, model_width)
    blended = lax.dot_general(
        blend, returned, (((0,), (0,)), ((), ())), preferred_element_type=jnp.float32
    )
    mixture = blended[:row_count] + blended[row_count:]
    finished = (attended.astype(jnp.float32) + mixture).astype(jnp.bfloat16)

    home_rows = lax.all_to_all(
        finished.reshape(cache_size, deal_rows, model_width), CACHE, 0, 0, tiled=True
    ).reshape(row_count, model_width)
    my_base = group_base + my_index * row_count
    sender_place = lax.dynamic_slice_in_dim(
        placing.reshape(cache_size, row_count), my_index * deal_rows, deal_rows, axis=1
    ).reshape(-1)
    to_row = (sender_place[None, :] - my_base == row_ids[:, None]).astype(jnp.bfloat16)
    mixed = jnp.dot(to_row, home_rows, preferred_element_type=jnp.float32).astype(jnp.bfloat16)
    from_group = (placing[None, :] - my_base == row_ids[:, None]).astype(jnp.bfloat16)
    cached = jnp.dot(from_group, kv_group, preferred_element_type=jnp.float32).astype(jnp.bfloat16)
    return (mixed, cached[:, :kv_width], cached[:, kv_width:])


def solution(mesh):
    fine = Mesh(np.asarray(mesh.devices).reshape(tuple(SIZES[a] for a in ALL)), ALL)
    in_specs = (
        P(ALL, None),
        P(DP),
        P(ALL),
        P(),
        P(ALL, None),
        P(ALL, None),
        P(),
        P(ALL, None),
        P(ALL, None),
        P(ALL, None, None),
        P(ALL, None, None),
    )
    out_specs = (P(ALL, None), P(ALL, None), P(ALL, None))
    return jax.shard_map(
        per_device, mesh=fine, in_specs=in_specs, out_specs=out_specs, check_vma=False
    )
```

time: 1180 us -> 461 us (0.39)
  waiting for transfers between devices: 775 us -> 232 us
  blocking collectives: 183 us -> 101 us
  local copies, waits for them, and re-layouts: 74.5 us -> 4.93 us
  other arithmetic: 42 us -> 9.55 us
  matrix products: 47.2 us -> 75.7 us
    all_gather x2, waiting for transfers between devices: 621 us -> 0.01 us  [the longest x1 0.01 us: per_device(): full_out = lax.all_gather(out_rows, DP, axis=0, tiled=True)]
    ppermute x0 -> x4, waiting for transfers between devices: none -> 134 us  [the longest x1 125 us: per_device(): other_down = lax.ppermute(w_down[0], ALL, pairs)]
    all_to_all x4 -> x3, waiting for transfers between devices: 153 us -> 98.6 us  [the longest x1 79.1 us: per_device(): lax.all_to_all(expert_out.reshape(CHIP_COUNT, MOST, model_width), CHIPS,...]
    all_gather x2 -> x0, blocking collectives: 44.9 us -> none  [the longest x1 23.9 us: per_device(): value_piece = lax.all_gather(values_here, 'cache', axis=0, tiled=True)]
    all_to_all x1 -> x3, blocking collectives: 138 us -> 101 us  [the longest x1 72.1 us: per_device(): lax.all_to_all(outgoing.reshape(CHIP_COUNT, MOST, model_width), CHIPS, 0,...]
    unnamed x20 -> x27, local copies, waits for them, and re-layouts: 28 us -> 0.13 us
    convert_element_type x6 -> x2, other arithmetic: 26.3 us -> 0.29 us  [the longest x1 0.2 us: per_device(): weighted_hi.astype(jnp.bfloat16)]
    all_to_all x4 -> x3, starting transfers between devices: 32 us -> 13.1 us  [the longest x1 5.82 us: per_device(): lax.all_to_all(expert_out.reshape(CHIP_COUNT, MOST, model_width), CHIPS,...]
  transfers between devices with their start and end apart: 6 -> 9, of which waited for: 5 -> 5; matrix products, arithmetic and copies ran while one was open for 7% -> 5% of each run, Pallas kernels for 0% -> 0%
where the time goes in v1:
time: 461 us; the launch traced here: 460 us
  waiting for transfers between devices  232 us (50%)
  blocking collectives  101 us (22%)
  matrix products  75.7 us (16%)
  starting transfers between devices  22.2 us (5%)
  between operations  14.4 us (3%)
  other arithmetic  9.55 us (2%)
  local copies, waits for them, and re-layouts  4.93 us (1%)
    ppermute x1, waiting for transfers between devices, per_device(): other_down = lax.ppermute(w_down[0], ALL, pairs)  125 us
    all_to_all x1, waiting for transfers between devices, per_device(): lax.all_to_all(expert_out.reshape(CHIP_COUNT, MOST, model_width), CHIPS,...  79.1 us
    all_to_all x1, blocking collectives, per_device(): lax.all_to_all(outgoing.reshape(CHIP_COUNT, MOST, model_width), CHIPS, 0,...  72.1 us
    dot_general x2, matrix products, expert_half(): joined = jnp.dot(rows, gate_up, preferred_element_type=jnp.float32)  30.3 us
    all_to_all x2, blocking collectives, spread(): lax.all_to_all(jnp.broadcast_to(shard[None], (count,) + shard.shape), axe...  29 us
    dot_general x2, matrix products, expert_half(): jnp.dot(active, down_part, preferred_element_type=jnp.float32)  20.2 us
    all_to_all x1, waiting for transfers between devices, per_device(): lax.all_to_all(finished.reshape(cache_size, deal_rows, model_width), CACH...  10.5 us
  transfers between devices with their start and end apart: 9, of which 5 were waited for; matrix products, arithmetic and copies ran while one was open for 5% of the time, Pallas kernels for 0%

profile of v1, /device:TPU:1, one launch (start us, length us, event | category | flops | bytes accessed | tf_op | source)
XLA Modules:
  0.0 460.1 jit_solution(13544084217098019637)
XLA Ops:
  8.2 16.5 %all_to_all.30 = bf16[8,10,2560]{2,1,0:T(8,128)(2,1)S(1)} all-to-all(bf16[8,10,2560]{2,1,0:T(8,128)(2,1)S(1)} %broadcast_in_dim.108), channel_id=1, replica_groups=mesh['yh'=2,'z'=4,'core'=2,'yl'=2,'x'=4] {'yl','x'}, dimensions={0} | all-to-all | bytes 819200 | tf_op jit(solution)/shard_map/all_to_all | solution.py:59
  25.7 12.5 %all_to_all.31 = bf16[8,20,1792]{2,1,0:T(8,128)(2,1)S(1)} all-to-all(bf16[8,20,1792]{2,1,0:T(8,128)(2,1)S(1)} %broadcast_in_dim.63), channel_id=1, replica_groups=mesh['yh'=2,'z'=4,'core'=2,'yl'=2,'x'=4] {'yl','x'}, dimensions={0} | all-to-all | bytes 1146880 | tf_op jit(solution)/shard_map/all_to_all | solution.py:59
  39.2 5.1 %collective-permute-start = (bf16[2560,1536]{1,0:T(8,128)(2,1)}, bf16[2560,1536]{1,0:T(8,128)(2,1)}, u32[]{:S(2)}, u32[]{:S(2)}) collective-permute-start(bf16[2560,1536]{1,0:T(8,128)(2,1)} %bitcast.175), channel_id=1, source_target_pairs={{8,1},{1,8},{10,3},{3,10},{12,5},{5,12},{14,7},{7,14},{24,17},{17,... | collective-permute-start | bytes 23592968 | tf_op jit(solution)/shard_map/ppermute | solution.py:94
  44.3 1.9 collective-permute-start.1
  47.2 125.0 %collective-permute-done.1 = bf16[768,2560]{1,0:T(8,128)(2,1)} collective-permute-done((bf16[768,2560]{1,0:T(8,128)(2,1)}, bf16[768,2560]{1,0:T(8,128)(2,1)}, u32[]{:S(2)}, u32[]{:S(2)}) %collective-permute-start.1) | collective-permute-done | bytes 3932192 | tf_op jit(solution)/shard_map/ppermute | solution.py:95
  172.2 5.0 %fusion.42 = f32[128,1792]{1,0:T(8,128)S(1)} fusion(bf16[2560,1792]{1,0:T(8,128)(2,1)} %all-gather.3.cloned.1.call-done, bf16[128,2560]{1,0:T(8,128)(2,1)S(1)} %copy-done, f32[2560]{0:T(1024)S(1)} %copy-done.2, f32[128]{0:T(128)S(1)} %add_rsqrt_fusion.1), kind=kOutput, calls=%fused_computation.55 | convolution fusion | flops 1175715840 | bytes 10758656 | tf_op jit(solution)/shard_map/dot_general | solution.py:132
  179.2 3.7 all-to-all-start.1
  189.6 9.0 %all-to-all-done.1 = bf16[8,128,512]{2,1,0:T(8,128)(2,1)S(1)} async-done(((bf16[8,128,512]{2,1,0:T(8,128)(2,1)}), bf16[8,128,512]{2,1,0:T(8,128)(2,1)S(1)}, u32[]{:S(2)}, u32[]{:S(2)}) %all-to-all-start.1) | async-done | bytes 1048608 | tf_op jit(solution)/shard_map/all_to_all | solution.py:59
  198.6 2.2 fusion.203
  200.8 2.3 fusion.35
  203.1 2.2 fusion.202
  205.3 2.3 fusion.38
  207.8 4.0 multiply_reduce_fusion
  213.4 72.1 %all_to_all.32 = bf16[64,16,2560]{2,1,0:T(8,128)(2,1)} all-to-all(bf16[64,16,2560]{2,1,0:T(8,128)(2,1)S(1)} %bitcast.165), channel_id=1, replica_groups=mesh['yh'=2,'z'=4,'core'=2,'yl'=2,'x'=4] {'yh','z','yl','x'}, dimensions={0} | all-to-all | bytes 10485760 | tf_op jit(solution)/shard_map/all_to_all | solution.py:178
  287.1 8.6 %collective-permute-done.2 = bf16[1024,2560]{1,0:T(8,128)(2,1)} collective-permute-done((bf16[1024,2560]{1,0:T(8,128)(2,1)}, bf16[1024,2560]{1,0:T(8,128)(2,1)}, u32[]{:S(2)}, u32[]{:S(2)}) %collective-permute-start.2) | collective-permute-done | bytes 5242912 | tf_op jit(solution)/shard_map/ppermute | solution.py:182
  295.7 15.1 %fusion.6 = f32[1024,1536]{1,0:T(8,128)} fusion(bf16[1024,2560]{1,0:T(8,128)(2,1)} %collective-permute-done.2, bf16[2560,1536]{1,0:T(8,128)(2,1)} %collective-permute-done, pred[]{:T(512)S(6)} %eq.80, bf16[1,2560,1536]{2,1,0:T(8,128)(2,1)} %param.20), kind=kOutput, calls=%fused_computation.16 | convolution fusion | flops 8056995840 | bytes 27262976 | tf_op jit(solution)/shard_map/dot_general | solution.py:65
  310.9 8.4 %convolution_convert_fusion = bf16[1024,2560]{1,0:T(8,128)(2,1)S(1)} fusion(f32[1024,1536]{1,0:T(8,128)} %fusion.6, bf16[768,2560]{1,0:T(8,128)(2,1)} %collective-permute-done.1, pred[]{:T(512)S(6)} %eq.80, bf16[1,768,2560]{2,1,0:T(8,128)(2,1)S(1)} %copy-done.8), kind=kOutput, calls=%fused_computation.4 | convolution fusion | flops 4035837952 | bytes 19398656 | tf_op jit(solution)/shard_map/dot_general | solution.py:68
  319.6 15.1 %fusion.7 = f32[1024,1536]{1,0:T(8,128)} fusion(bf16[1024,2560]{1,0:T(8,128)(2,1)} %bitcast.43, bf16[2560,1536]{1,0:T(8,128)(2,1)} %collective-permute-done, pred[]{:T(512)S(6)} %eq.80, bf16[1,2560,1536]{2,1,0:T(8,128)(2,1)} %param.20), kind=kOutput, calls=%fused_computation.17 | convolution fusion | flops 8056995840 | bytes 27262976 | tf_op jit(solution)/shard_map/dot_general | solution.py:65
  334.7 11.9 %add_convert_fusion = bf16[1024,2560]{1,0:T(8,128)(2,1)} fusion(bf16[1024,2560]{1,0:T(8,128)(2,1)S(1)} %collective-permute-done.3, f32[1024,1536]{1,0:T(8,128)} %fusion.7, bf16[768,2560]{1,0:T(8,128)(2,1)} %collective-permute-done.1, pred[]{:T(512)S(6)} %eq.80, bf16[1,768,2560]{2,1,0:T(8,128)(2,1)} %param.21), kind=kOutput, calls=%fused_computation.2 | convolution fusion | flops 4046323712 | bytes 24641536 | tf_op jit(solution)/shard_map/dot_general | solution.py:68
  346.6 5.8 %all-to-all-start.4 = ((bf16[64,16,2560]{2,1,0:T(8,128)(2,1)}), bf16[64,16,2560]{2,1,0:T(8,128)(2,1)}, u32[]{:S(2)}, u32[]{:S(2)}) async-start(bf16[64,16,2560]{2,1,0:T(8,128)(2,1)} %bitcast.166), calls=%async_computation.4 | async-start | bytes 10485760 | tf_op jit(solution)/shard_map/all_to_all | solution.py:189
  352.7 79.1 %all-to-all-done.4 = bf16[64,16,2560]{2,1,0:T(8,128)(2,1)} async-done(((bf16[64,16,2560]{2,1,0:T(8,128)(2,1)}), bf16[64,16,2560]{2,1,0:T(8,128)(2,1)}, u32[]{:S(2)}, u32[]{:S(2)}) %all-to-all-start.4) | async-done | bytes 5242912 | tf_op jit(solution)/shard_map/all_to_all | solution.py:189
  431.8 4.0 fusion.49
  436.9 3.5 all-to-all-start.5
  441.6 10.5 %all-to-all-done.5 = bf16[8,16,2560]{2,1,0:T(8,128)(2,1)S(1)} async-done(((bf16[8,16,2560]{2,1,0:T(8,128)(2,1)}), bf16[8,16,2560]{2,1,0:T(8,128)(2,1)S(1)}, u32[]{:S(2)}, u32[]{:S(2)}) %all-to-all-start.5) | async-done | bytes 655392 | tf_op jit(solution)/shard_map/all_to_all | solution.py:198
  (79 shorter events, 19.8 us)
Async XLA Ops:
  7.2 18.5 %copy-start.1 = (bf16[20,1792]{1,0:T(8,128)(2,1)S(1)}, bf16[20,1792]{1,0:T(8,128)(2,1)}, u32[]{:S(2)}) copy-start(bf16[20,1792]{1,0:T(8,128)(2,1)} %param.15) | copy-start | bytes 215044
  7.2 165.0 %all-gather.5.cloned.1.call-start = ((), (), s32[]{:S(2)}) async-start(), calls=%async_computation.7 | async-start | bytes 6963200 | tf_op jit(solution)/shard_map/all_gather | solution.py:101
  8.2 38.1 %copy-start.6 = (s32[128,6]{0,1:T(8,128)S(1)}, s32[128,6]{0,1:T(8,128)}, u32[]{:S(2)}) copy-start(s32[128,6]{0,1:T(8,128)} %param.18) | copy-start | bytes 9220
  24.7 22.0 %copy-start = (bf16[128,2560]{1,0:T(8,128)(2,1)S(1)}, bf16[128,2560]{1,0:T(8,128)(2,1)}, u32[]{:S(2)}) copy-start(bf16[128,2560]{1,0:T(8,128)(2,1)} %param.11) | copy-start | bytes 1966084
  24.7 22.3 %copy-start.3 = (s32[1024]{0:T(1024)S(1)}, s32[1024]{0:T(1024)}, u32[]{:S(2)}) copy-start(s32[1024]{0:T(1024)} %param.12) | copy-start | bytes 12292
  24.7 22.3 %copy-start.7 = (s32[128]{0:T(128)S(1)}, s32[128]{0:T(128)}, u32[]{:S(2)}) copy-start(s32[128]{0:T(128)} %param.13) | copy-start | bytes 1540
  24.7 147.5 %copy-start.2 = (f32[2560]{0:T(1024)S(1)}, f32[2560]{0:T(1024)}, u32[]{:S(2)}) copy-start(f32[2560]{0:T(1024)} %param.14) | copy-start | bytes 30724
  25.6 146.6 %all-gather.3.cloned.1.call-start = ((), (), s32[]{:S(2)}) async-start(), calls=%async_computation.6 | async-start | bytes 9748480 | tf_op jit(solution)/shard_map/all_gather | solution.py:99
  39.2 133.0 %collective-permute-start = (bf16[2560,1536]{1,0:T(8,128)(2,1)}, bf16[2560,1536]{1,0:T(8,128)(2,1)}, u32[]{:S(2)}, u32[]{:S(2)}) collective-permute-start(bf16[2560,1536]{1,0:T(8,128)(2,1)} %bitcast.175), channel_id=1, source_target_pairs={{8,1},{1,8},{10,3},{3,10},{12,5},{5,12},{14,7},{7,14},{24,17},{17,... | collective-permute-start | bytes 23592968 | tf_op jit(solution)/shard_map/ppermute | solution.py:94
  44.3 127.9 %collective-permute-start.1 = (bf16[768,2560]{1,0:T(8,128)(2,1)}, bf16[768,2560]{1,0:T(8,128)(2,1)}, u32[]{:S(2)}, u32[]{:S(2)}) collective-permute-start(bf16[768,2560]{1,0:T(8,128)(2,1)} %bitcast.176), channel_id=1, source_target_pairs={{8,1},{1,8},{10,3},{3,10},{12,5},{5,12},{14,7},{7,14},{24,17},{17,... | collective-permute-start | bytes 11796488 | tf_op jit(solution)/shard_map/ppermute | solution.py:95
  179.2 19.4 %all-to-all-start.1 = ((bf16[8,128,512]{2,1,0:T(8,128)(2,1)}), bf16[8,128,512]{2,1,0:T(8,128)(2,1)S(1)}, u32[]{:S(2)}, u32[]{:S(2)}) async-start(bf16[8,128,512]{2,1,0:T(8,128)(2,1)} %broadcast_in_dim.64), calls=%async_computation.1 | async-start | bytes 2097152 | tf_op jit(solution)/shard_map/all_to_all | solution.py:59
  207.7 4.0 copy-start.4
  285.5 10.3 %collective-permute-start.2 = (bf16[1024,2560]{1,0:T(8,128)(2,1)}, bf16[1024,2560]{1,0:T(8,128)(2,1)}, u32[]{:S(2)}, u32[]{:S(2)}) collective-permute-start(bf16[1024,2560]{1,0:T(8,128)(2,1)} %bitcast.43), channel_id=1, source_target_pairs={{0,8},{8,0},{1,9},{9,1},{2,10},{10,2},{3,11},{11,3},{4,12},{12,4},... | collective-permute-start | bytes 15728648 | tf_op jit(solution)/shard_map/ppermute | solution.py:182
  287.1 23.7 %copy-start.8 = (bf16[1,768,2560]{2,1,0:T(8,128)(2,1)S(1)}, bf16[1,768,2560]{2,1,0:T(8,128)(2,1)}, u32[]{:S(2)}) copy-start(bf16[1,768,2560]{2,1,0:T(8,128)(2,1)} %param.21) | copy-start | bytes 11796484
  319.2 15.5 %collective-permute-start.3 = (bf16[1024,2560]{1,0:T(8,128)(2,1)S(1)}, bf16[1024,2560]{1,0:T(8,128)(2,1)S(1)}, u32[]{:S(2)}, u32[]{:S(2)}) collective-permute-start(bf16[1024,2560]{1,0:T(8,128)(2,1)S(1)} %convolution_convert_fusion), channel_id=1, source_target_pairs={{0,8},{8,0},{1,9},{9,1},{2,10},{10,2},{3,11},{11,3},{4,12},{12,4},... | collective-permute-start | bytes 15728648 | tf_op jit(solution)/shard_map/ppermute | solution.py:186
  346.6 5.8 %copy-start.5 = (f32[128,6]{0,1:T(8,128)S(1)}, f32[128,6]{0,1:T(8,128)}, u32[]{:S(2)}) copy-start(f32[128,6]{0,1:T(8,128)} %param.19) | copy-start | bytes 9220
  346.6 85.2 %all-to-all-start.4 = ((bf16[64,16,2560]{2,1,0:T(8,128)(2,1)}), bf16[64,16,2560]{2,1,0:T(8,128)(2,1)}, u32[]{:S(2)}, u32[]{:S(2)}) async-start(bf16[64,16,2560]{2,1,0:T(8,128)(2,1)} %bitcast.166), calls=%async_computation.4 | async-start | bytes 10485760 | tf_op jit(solution)/shard_map/all_to_all | solution.py:189
  436.9 15.2 %all-to-all-start.5 = ((bf16[8,16,2560]{2,1,0:T(8,128)(2,1)}), bf16[8,16,2560]{2,1,0:T(8,128)(2,1)S(1)}, u32[]{:S(2)}, u32[]{:S(2)}) async-start(bf16[8,16,2560]{2,1,0:T(8,128)(2,1)} %bitcast.46), calls=%async_computation.5 | async-start | bytes 1310720 | tf_op jit(solution)/shard_map/all_to_all | solution.py:198
Sparse Core Ops, SparseCore 0:
  25.7 67.0 all-gather.4
  95.9 74.1 all-gather.2

commit v2 on v1

--- a/solution.py
+++ b/solution.py
@@ -59,6 +59,44 @@
     return lax.all_to_all(
         jnp.broadcast_to(shard[None], (count,) + shard.shape), axes, 0, 0, tiled=True
     )
+
+
+def ring(block, axes):
+    half = block.shape[0] // 2
+    upward = [(i, (i + 1) % 4) for i in range(4)]
+    downward = [(i, (i - 1) % 4) for i in range(4)]
+    below = lax.ppermute(block, axes, upward)
+    above = lax.ppermute(block, axes, downward)
+    far_low = lax.ppermute(below[:half], axes, upward)
+    far_high = lax.ppermute(above[half:], axes, downward)
+    return jnp.concatenate([block, below, above, far_low, far_high], axis=0)
+
+
+RING_Y = ("yh", "yl")
+STEPS = (0, -1, 1, 2)
+CORES = [(0, 1), (1, 0)]
+
+
+def source_features(block_rows, y_outer, flip):
+    count = 16 * block_rows
+    index = jnp.arange(count, dtype=jnp.int32)
+    offsets = jnp.array(STEPS, jnp.int32)
+    outer = offsets[index // (4 * block_rows)]
+    inner = offsets[index // block_rows % 4]
+    dy, dz = (outer, inner) if y_outer else (inner, outer)
+    y = (lax.axis_index(RING_Y) + dy) % 4
+    z = (lax.axis_index("z") + dz) % 4
+    core = lax.axis_index("core")
+    core = 1 - core if flip else core
+    block = (((y // 2) * 4 + z) * 2 + core) * 2 + y % 2
+    return block * block_rows + index % block_rows
+
+
+def reordered(features, order):
+    count = features.shape[1]
+    ids = jnp.arange(count, dtype=jnp.int32)
+    take = (ids[:, None] == order[None, :]).astype(jnp.bfloat16)
+    return jnp.dot(features, take, preferred_element_type=jnp.float32).astype(jnp.bfloat16)
 
 
 def expert_half(rows, gate_up, down_part):
@@ -91,16 +129,23 @@
     group_base = lax.axis_index(DP) * group_rows
 
     pairs = swap_pairs()
-    other_up = lax.ppermute(w_gate_up[0], ALL, pairs)
+    up_rows = w_gate_up.shape[1] // 2
+    other_low = lax.ppermute(w_gate_up[0, :up_rows], ALL, pairs)
+    other_high = lax.ppermute(w_gate_up[0, up_rows:], ALL, pairs)
     other_down = lax.ppermute(w_down[0], ALL, pairs)
     keep = lax.axis_index("x") % 2 == lax.axis_index("core")
 
-    qkv_rows = spread(w_qkv, CACHE, cache_size).reshape(-1, w_qkv.shape[1])
-    full_qkv = lax.all_gather(qkv_rows, DP, axis=0, tiled=True)
+    block = spread(w_qkv, "x", 4).reshape(-1, w_qkv.shape[1])
+    block_rows = block.shape[0]
+    half_width = block.shape[1] // 2
+    first = ring(ring(block[:, :half_width], "z"), RING_Y)
+    last = ring(ring(block[:, half_width:], RING_Y), "z")
+    last_other = lax.ppermute(last, "core", CORES)
+    first_other = lax.ppermute(first, "core", CORES)
     out_rows = spread(w_out, CACHE, cache_size).reshape(-1, w_out.shape[1])
     full_out = lax.all_gather(out_rows, DP, axis=0, tiled=True)
-    full_qkv, other_up = lax.optimization_barrier((full_qkv, other_up))
-    full_out, other_down = lax.optimization_barrier((full_out, other_down))
+    last_other, other_low = lax.optimization_barrier((last_other, other_low))
+    full_out, other_high = lax.optimization_barrier((full_out, other_high))
 
     my_place = lax.dynamic_slice_in_dim(placing, my_index * row_count, row_count)
     position = my_place - prompt_start
@@ -129,7 +174,15 @@
     blend = jnp.concatenate([weighted_hi.astype(jnp.bfloat16), weighted_lo], axis=1)
 
     normed = rms_scaled(hidden_in, attn_gain)
-    projected = jnp.dot(normed, full_qkv, preferred_element_type=jnp.float32)
+    def project(own, other, y_outer):
+        part = reordered(normed, source_features(block_rows, y_outer, False))
+        total = jnp.dot(part, own, preferred_element_type=jnp.float32)
+        part = reordered(normed, source_features(block_rows, y_outer, True))
+        return total + jnp.dot(part, other, preferred_element_type=jnp.float32)
+
+    projected = jnp.concatenate(
+        [project(first, first_other, True), project(last, last_other, False)], axis=1
+    )
     half_size = HD // 2
     inverse = rope_base ** (-(jnp.arange(half_size, dtype=jnp.float32) * 2.0 / HD))
     angles = position.astype(jnp.float32)[:, None] * inverse[None, :]
@@ -178,12 +231,11 @@
     mine = lax.all_to_all(
         outgoing.reshape(CHIP_COUNT, MOST, model_width), CHIPS, 0, 0, tiled=True
     ).reshape(CHIP_COUNT * MOST, model_width)
-    cores = [(0, 1), (1, 0)]
-    mates = lax.ppermute(mine, "core", cores)
-    gate_up = jnp.where(keep, w_gate_up[0], other_up)
+    mates = lax.ppermute(mine, "core", CORES)
+    gate_up = jnp.where(keep, w_gate_up[0], jnp.concatenate([other_low, other_high], axis=0))
     down_part = jnp.where(keep, w_down[0], other_down)
     for_mate = expert_half(mates, gate_up, down_part)
-    from_mate = lax.ppermute(for_mate, "core", cores)
+    from_mate = lax.ppermute(for_mate, "core", CORES)
     own_part = expert_half(mine, gate_up, down_part)
     expert_out = (own_part.astype(jnp.float32) + from_mate.astype(jnp.float32)).astype(jnp.bfloat16)
     returned = lax.all_to_all(

time: 461 us -> 475 us (1.030); the launches traced: 460 us -> 468 us
  waiting for transfers between devices: 232 us -> 180 us
  starting transfers between devices: 22.2 us -> 61.2 us
  local copies, waits for them, and re-layouts: 4.93 us -> 24.2 us
  matrix products: 75.7 us -> 90.9 us
  blocking collectives: 101 us -> 87.7 us
    ppermute x1, waiting for transfers between devices: 125 us -> 25.8 us  [per_device(): other_down = lax.ppermute(w_down[0], ALL, pairs)]
    ppermute x3 -> x22, waiting for transfers between devices: 8.63 us -> 60.3 us  [the longest x4 26.1 us: ring(): below = lax.ppermute(block, axes, upward)]
    ppermute x3 -> x22, starting transfers between devices: 7.08 us -> 42.6 us  [the longest x4 10 us: ring(): far_high = lax.ppermute(above[half:], axes, downward)]
    dot_general x1 -> x4, matrix products: 5.04 us -> 30.1 us  [the longest x2 20.4 us: project(): total = jnp.dot(part, own, preferred_element_type=jnp.float32)]
    all_to_all x2 -> x1, blocking collectives: 29 us -> 16.5 us  [spread(): lax.all_to_all(jnp.broadcast_to(shard[None], (count,) + shard.shape), axe...]
    all_to_all x1, waiting for transfers between devices: 79.1 us -> 69 us  [per_device(): lax.all_to_all(expert_out.reshape(CHIP_COUNT, MOST, model_width), CHIPS,...]
    unnamed x27 -> x36, local copies, waits for them, and re-layouts: 0.13 us -> 10.1 us
    all_to_all x1 -> x2, waiting for transfers between devices: 8.98 us -> 15 us  [spread(): lax.all_to_all(jnp.broadcast_to(shard[None], (count,) + shard.shape), axe...]
  transfers between devices with their start and end apart: 9 -> 28, of which waited for: 5 -> 14; matrix products, arithmetic and copies ran while one was open for 5% -> 21% of each run, Pallas kernels for 0% -> 0%
where the time goes in v2:
time: 475 us; the launch traced here: 468 us
  waiting for transfers between devices  180 us (38%)
  matrix products  90.9 us (19%)
  blocking collectives  87.7 us (18%)
  starting transfers between devices  61.2 us (13%)
  local copies, waits for them, and re-layouts  24.2 us (5%)
  between operations  15 us (3%)
  other arithmetic  8.19 us (2%)
    all_to_all x1, blocking collectives, per_device(): lax.all_to_all(outgoing.reshape(CHIP_COUNT, MOST, model_width), CHIPS, 0,...  71.2 us
    all_to_all x1, waiting for transfers between devices, per_device(): lax.all_to_all(expert_out.reshape(CHIP_COUNT, MOST, model_width), CHIPS,...  69 us
    dot_general x2, matrix products, expert_half(): joined = jnp.dot(rows, gate_up, preferred_element_type=jnp.float32)  27 us
    ppermute x4, waiting for transfers between devices, ring(): below = lax.ppermute(block, axes, upward)  26.1 us
    ppermute x1, waiting for transfers between devices, per_device(): other_down = lax.ppermute(w_down[0], ALL, pairs)  25.8 us
    dot_general x2, matrix products, project(): total = jnp.dot(part, own, preferred_element_type=jnp.float32)  20.4 us
    dot_general x2, matrix products, expert_half(): jnp.dot(active, down_part, preferred_element_type=jnp.float32)  17.3 us
    all_to_all x1, blocking collectives, spread(): lax.all_to_all(jnp.broadcast_to(shard[None], (count,) + shard.shape), axe...  16.5 us
  transfers between devices with their start and end apart: 28, of which 14 were waited for; matrix products, arithmetic and copies ran while one was open for 21% of the time, Pallas kernels for 0%

profile of v2, /device:TPU:1, one launch (start us, length us, event | category | flops | bytes accessed | tf_op | source)
XLA Modules:
  0.0 467.6 jit_solution(4816341207152578532)
XLA Ops:
  8.1 16.5 %all_to_all.30 = bf16[8,10,2560]{2,1,0:T(8,128)(2,1)S(1)} all-to-all(bf16[8,10,2560]{2,1,0:T(8,128)(2,1)S(1)} %broadcast_in_dim.63), channel_id=1, replica_groups=mesh['yh'=2,'z'=4,'core'=2,'yl'=2,'x'=4] {'yl','x'}, dimensions={0} | all-to-all | bytes 819200 | tf_op jit(solution)/shard_map/all_to_all | solution.py:59
  30.7 5.6 %slice_bitcast_fusion = (bf16[1280,1536]{1,0:T(8,128)(2,1)}, bf16[1280,1536]{1,0:T(8,128)(2,1)}) fusion(bf16[1,2560,1536]{2,1,0:T(8,128)(2,1)} %param.24), kind=kLoop, calls=%fused_computation.30 | loop fusion | bytes 15728640 | tf_op jit(solution)/shard_map/squeeze | solution.py:134
  36.3 5.2 %collective-permute-start.18 = (bf16[1280,1536]{1,0:T(8,128)(2,1)}, bf16[1280,1536]{1,0:T(8,128)(2,1)}, u32[]{:S(2)}, u32[]{:S(2)}) collective-permute-start(bf16[1280,1536]{1,0:T(8,128)(2,1)} %get-tuple-element.18), channel_id=1, source_target_pairs={{8,1},{1,8},{10,3},{3,10},{12,5},{5,12},{14,7},{7,14},{24,17},{17,... | collective-permute-start | bytes 11796488 | tf_op jit(solution)/shard_map/ppermute | solution.py:133
  63.1 22.8 %collective-permute-done.9 = bf16[80,896]{1,0:T(8,128)(2,1)S(1)} collective-permute-done((bf16[80,896]{1,0:T(8,128)(2,1)S(1)}, bf16[80,896]{1,0:T(8,128)(2,1)S(1)}, u32[]{:S(2)}, u32[]{:S(2)}) %collective-permute-start.9) | collective-permute-done | bytes 143392 | tf_op jit(solution)/shard_map/ppermute | solution.py:68
  89.4 6.8 %collective-permute-done.11 = bf16[40,896]{1,0:T(8,128)(2,1)S(1)} collective-permute-done((bf16[40,896]{1,0:T(8,128)(2,1)S(1)}, bf16[40,896]{1,0:T(8,128)(2,1)S(1)}, u32[]{:S(2)}, u32[]{:S(2)}) %collective-permute-start.11) | collective-permute-done | bytes 71712 | tf_op jit(solution)/shard_map/ppermute | solution.py:70
  109.5 8.1 %collective-permute-start.8 = (bf16[1280,896]{1,0:T(8,128)(2,1)}, bf16[1280,896]{1,0:T(8,128)(2,1)}, u32[]{:S(2)}, u32[]{:S(2)}) collective-permute-start(bf16[1280,896]{1,0:T(8,128)(2,1)} %constant_dynamic-update-slice_fusion.5), channel_id=1, source_target_pairs={{0,8},{8,0},{1,9},{9,1},{2,10},{10,2},{3,11},{11,3},{4,12},{12,4},... | collective-permute-start | bytes 6881288 | tf_op jit(solution)/shard_map/ppermute | solution.py:144
  121.4 12.0 %collective-permute-done.14 = bf16[320,896]{1,0:T(8,128)(2,1)S(1)} collective-permute-done((bf16[320,896]{1,0:T(8,128)(2,1)}, bf16[320,896]{1,0:T(8,128)(2,1)S(1)}, u32[]{:S(2)}, u32[]{:S(2)}) %collective-permute-start.14) | collective-permute-done | bytes 573472 | tf_op jit(solution)/shard_map/ppermute | solution.py:69
  145.1 4.8 %fusion.63 = f32[128,896]{1,0:T(8,128)S(1)} fusion(bf16[1280,896]{1,0:T(8,128)(2,1)} %collective-permute-done.8, s32[1280]{0:T(1024)S(1)} %multiply_add_fusion.2, bf16[128,2560]{1,0:T(8,128)(2,1)S(1)} %copy-done, f32[2560]{0:T(1024)S(1)} %copy-done.6, f32[128]{0:T(128)S(1)} %add_rsqrt_fusion.1), kind=kOutput, calls=%fused_computation.82 | convolution fusion | flops 1137213440 | bytes 3423744 | tf_op jit(solution)/shard_map/dot_general | solution.py:181
  150.0 4.8 %convolution_add_fusion.2 = f32[128,896]{1,0:T(8,128)S(1)} fusion(f32[128,896]{1,0:T(8,128)S(1)} %fusion.63, bf16[1280,896]{1,0:T(8,128)(2,1)} %constant_dynamic-update-slice_fusion.5, s32[1280]{0:T(1024)S(1)} %get-tuple-element.15, bf16[128,2560]{1,0:T(8,128)(2,1)S(1)} %copy-done, f32[2560]{0:T(1024)S(1)} %copy-done.6, f32[128]{0:T(128)S(1)} %add_rsqrt_fusion.1), kind=kOutput, calls=%fused_computation.74 | convolution fusion | flops 1137328128 | bytes 3882496 | tf_op jit(solution)/shard_map/dot_general | solution.py:179
  155.3 4.8 %fusion.64 = f32[128,896]{1,0:T(8,128)S(1)} fusion(bf16[1280,896]{1,0:T(8,128)(2,1)} %collective-permute-done.17, s32[1280]{0:T(1024)S(1)} %multiply_add_fusion, bf16[128,2560]{1,0:T(8,128)(2,1)S(1)} %copy-done, f32[2560]{0:T(1024)S(1)} %copy-done.6, f32[128]{0:T(128)S(1)} %add_rsqrt_fusion.1), kind=kOutput, calls=%fused_computation.83 | convolution fusion | flops 1137213440 | bytes 3423744 | tf_op jit(solution)/shard_map/dot_general | solution.py:181
  160.2 15.6 %convolution_add_fusion.1 = f32[128,896]{1,0:T(8,128)S(1)} fusion(f32[128,896]{1,0:T(8,128)S(1)} %fusion.64, bf16[1280,896]{1,0:T(8,128)(2,1)} %constant_dynamic-update-slice_fusion.24, s32[1280]{0:T(1024)S(1)} %get-tuple-element.11, bf16[128,2560]{1,0:T(8,128)(2,1)S(1)} %copy-done, f32[2560]{0:T(1024)S(1)} %copy-done.6, f32[128]{0:T(128)S(1)} %add_rsqrt_fusion.1), kind=kOutput, calls=%fused_computation.73 | convolution fusion | flops 1137328128 | bytes 3882496 | tf_op jit(solution)/shard_map/dot_general | solution.py:179
  182.2 15.0 %all-to-all-done.1 = bf16[8,128,512]{2,1,0:T(8,128)(2,1)S(1)} async-done(((bf16[8,128,512]{2,1,0:T(8,128)(2,1)}), bf16[8,128,512]{2,1,0:T(8,128)(2,1)S(1)}, u32[]{:S(2)}, u32[]{:S(2)}) %all-to-all-start.1) | async-done | bytes 1048608 | tf_op jit(solution)/shard_map/all_to_all | solution.py:59
  202.7 4.0 multiply_reduce_fusion
  208.3 71.2 %all_to_all.31 = bf16[64,16,2560]{2,1,0:T(8,128)(2,1)} all-to-all(bf16[64,16,2560]{2,1,0:T(8,128)(2,1)S(1)} %bitcast.173), channel_id=1, replica_groups=mesh['yh'=2,'z'=4,'core'=2,'yl'=2,'x'=4] {'yh','z','yl','x'}, dimensions={0} | all-to-all | bytes 10485760 | tf_op jit(solution)/shard_map/all_to_all | solution.py:231
  283.3 6.5 %collective-permute-done.21 = bf16[1024,2560]{1,0:T(8,128)(2,1)} collective-permute-done((bf16[1024,2560]{1,0:T(8,128)(2,1)}, bf16[1024,2560]{1,0:T(8,128)(2,1)}, u32[]{:S(2)}, u32[]{:S(2)}) %collective-permute-start.21) | collective-permute-done | bytes 5242912 | tf_op jit(solution)/shard_map/ppermute | solution.py:234
  289.8 12.9 %fusion.11 = f32[1024,1536]{1,0:T(8,128)S(1)} fusion(bf16[1024,2560]{1,0:T(8,128)(2,1)} %collective-permute-done.21, bf16[1280,1536]{1,0:T(8,128)(2,1)} %collective-permute-done.19, bf16[1280,1536]{1,0:T(8,128)(2,1)} %collective-permute-done.18, bf16[1,2560,1536]{2,1,0:T(8,128)(2,1)} %param.24, pred[]{:T(512)S(6)} %eq.165), kind=kOutput, calls=%fused_computation.17 | convolution fusion | flops 8072724480 | bytes 27262976 | tf_op jit(solution)/shard_map/dot_general | solution.py:103
  302.7 25.8 %collective-permute-done.20 = bf16[768,2560]{1,0:T(8,128)(2,1)} collective-permute-done((bf16[768,2560]{1,0:T(8,128)(2,1)}, bf16[768,2560]{1,0:T(8,128)(2,1)}, u32[]{:S(2)}, u32[]{:S(2)}) %collective-permute-start.20) | collective-permute-done | bytes 3932192 | tf_op jit(solution)/shard_map/ppermute | solution.py:135
  328.5 7.9 %convolution_convert_fusion = bf16[1024,2560]{1,0:T(8,128)(2,1)S(1)} fusion(f32[1024,1536]{1,0:T(8,128)S(1)} %fusion.11, bf16[768,2560]{1,0:T(8,128)(2,1)} %collective-permute-done.20, pred[]{:T(512)S(6)} %eq.165, bf16[1,768,2560]{2,1,0:T(8,128)(2,1)} %param.25), kind=kOutput, calls=%fused_computation.27 | convolution fusion | flops 4035837952 | bytes 19398656 | tf_op jit(solution)/shard_map/dot_general | solution.py:106
  336.7 14.1 %fusion.7 = f32[1024,1536]{1,0:T(8,128)} fusion(bf16[1024,2560]{1,0:T(8,128)(2,1)} %bitcast.43, bf16[1,2560,1536]{2,1,0:T(8,128)(2,1)} %param.24, bf16[1,1280,1536]{2,1,0:T(8,128)(2,1)} %bitcast.45, bf16[1,1280,1536]{2,1,0:T(8,128)(2,1)} %bitcast.44, pred[]{:T(512)S(6)} %eq.165), kind=kOutput, calls=%fused_computation.13 | convolution fusion | flops 8072724480 | bytes 27262976 | tf_op jit(solution)/shard_map/dot_general | solution.py:103
  350.8 9.4 %convolution_convert_fusion.1 = bf16[1024,2560]{1,0:T(8,128)(2,1)S(1)} fusion(f32[1024,1536]{1,0:T(8,128)} %fusion.7, bf16[768,2560]{1,0:T(8,128)(2,1)} %collective-permute-done.20, pred[]{:T(512)S(6)} %eq.165, bf16[1,768,2560]{2,1,0:T(8,128)(2,1)} %param.25), kind=kOutput, calls=%fused_computation.28 | convolution fusion | flops 4035837952 | bytes 19398656 | tf_op jit(solution)/shard_map/dot_general | solution.py:106
  363.9 5.8 %all-to-all-start.4 = ((bf16[64,16,2560]{2,1,0:T(8,128)(2,1)}), bf16[64,16,2560]{2,1,0:T(8,128)(2,1)}, u32[]{:S(2)}, u32[]{:S(2)}) async-start(bf16[64,16,2560]{2,1,0:T(8,128)(2,1)} %bitcast.174), calls=%async_computation.4 | async-start | bytes 10485760 | tf_op jit(solution)/shard_map/all_to_all | solution.py:241
  370.1 69.0 %all-to-all-done.4 = bf16[64,16,2560]{2,1,0:T(8,128)(2,1)} async-done(((bf16[64,16,2560]{2,1,0:T(8,128)(2,1)}), bf16[64,16,2560]{2,1,0:T(8,128)(2,1)}, u32[]{:S(2)}, u32[]{:S(2)}) %all-to-all-start.4) | async-done | bytes 5242912 | tf_op jit(solution)/shard_map/all_to_all | solution.py:241
  439.1 4.0 fusion.68
  449.0 10.2 %all-to-all-done.5 = bf16[8,16,2560]{2,1,0:T(8,128)(2,1)S(1)} async-done(((bf16[8,16,2560]{2,1,0:T(8,128)(2,1)}), bf16[8,16,2560]{2,1,0:T(8,128)(2,1)S(1)}, u32[]{:S(2)}, u32[]{:S(2)}) %all-to-all-start.5) | async-done | bytes 655392 | tf_op jit(solution)/shard_map/all_to_all | solution.py:250
  (149 shorter events, 89.6 us)
Async XLA Ops:
  26.2 15.3 %all-to-all-start = ((bf16[4,20,1792]{2,1,0:T(8,128)(2,1)}), bf16[4,20,1792]{2,1,0:T(8,128)(2,1)S(1)}, u32[]{:S(2)}, u32[]{:S(2)}) async-start(bf16[4,20,1792]{2,1,0:T(8,128)(2,1)} %broadcast_in_dim.59), calls=%async_computation | async-start | bytes 688128 | tf_op jit(solution)/shard_map/all_to_all | solution.py:59
  29.7 173.0 %all-gather.2.cloned.1.call-start = ((), (), s32[]{:S(2)}) async-start(), calls=%async_computation.6 | async-start | bytes 6963200 | tf_op jit(solution)/shard_map/all_gather | solution.py:146
  36.3 119.1 %collective-permute-start.18 = (bf16[1280,1536]{1,0:T(8,128)(2,1)}, bf16[1280,1536]{1,0:T(8,128)(2,1)}, u32[]{:S(2)}, u32[]{:S(2)}) collective-permute-start(bf16[1280,1536]{1,0:T(8,128)(2,1)} %get-tuple-element.18), channel_id=1, source_target_pairs={{8,1},{1,8},{10,3},{3,10},{12,5},{5,12},{14,7},{7,14},{24,17},{17,... | collective-permute-start | bytes 11796488 | tf_op jit(solution)/shard_map/ppermute | solution.py:133
  44.1 7.3 %collective-permute-start.1 = (bf16[80,896]{1,0:T(8,128)(2,1)S(1)}, bf16[80,896]{1,0:T(8,128)(2,1)S(1)}, u32[]{:S(2)}, u32[]{:S(2)}) collective-permute-start(bf16[80,896]{1,0:T(8,128)(2,1)S(1)} %get-tuple-element.48), channel_id=1, source_target_pairs={{0,48},{16,0},{32,16},{48,32},{1,49},{17,1},{33,17},{49,33},{2,50}... | collective-permute-start | bytes 430088 | tf_op jit(solution)/shard_map/ppermute | solution.py:69
  58.7 38.2 %collective-permute-start.4 = (bf16[320,896]{1,0:T(8,128)(2,1)}, bf16[320,896]{1,0:T(8,128)(2,1)S(1)}, u32[]{:S(2)}, u32[]{:S(2)}) collective-permute-start(bf16[320,896]{1,0:T(8,128)(2,1)} %get-tuple-element.63), channel_id=1, source_target_pairs={{0,4},{4,64},{64,68},{68,0},{1,5},{5,65},{65,69},{69,1},{2,6},{6,6... | collective-permute-start | bytes 1720328 | tf_op jit(solution)/shard_map/ppermute | solution.py:68
  58.7 27.2 %collective-permute-start.9 = (bf16[80,896]{1,0:T(8,128)(2,1)S(1)}, bf16[80,896]{1,0:T(8,128)(2,1)S(1)}, u32[]{:S(2)}, u32[]{:S(2)}) collective-permute-start(bf16[80,896]{1,0:T(8,128)(2,1)S(1)} %get-tuple-element.47), channel_id=1, source_target_pairs={{0,4},{4,64},{64,68},{68,0},{1,5},{5,65},{65,69},{69,1},{2,6},{6,6... | collective-permute-start | bytes 430088 | tf_op jit(solution)/shard_map/ppermute | solution.py:68
  60.0 27.8 %collective-permute-start.10 = (bf16[80,896]{1,0:T(8,128)(2,1)S(1)}, bf16[80,896]{1,0:T(8,128)(2,1)S(1)}, u32[]{:S(2)}, u32[]{:S(2)}) collective-permute-start(bf16[80,896]{1,0:T(8,128)(2,1)S(1)} %get-tuple-element.47), channel_id=1, source_target_pairs={{0,68},{4,0},{64,4},{68,64},{1,69},{5,1},{65,5},{69,65},{2,70},{6,... | collective-permute-start | bytes 430088 | tf_op jit(solution)/shard_map/ppermute | solution.py:69
  61.5 39.8 %collective-permute-start.5 = (bf16[320,896]{1,0:T(8,128)(2,1)}, bf16[320,896]{1,0:T(8,128)(2,1)S(1)}, u32[]{:S(2)}, u32[]{:S(2)}) collective-permute-start(bf16[320,896]{1,0:T(8,128)(2,1)} %get-tuple-element.63), channel_id=1, source_target_pairs={{0,68},{4,0},{64,4},{68,64},{1,69},{5,1},{65,5},{69,65},{2,70},{6,... | collective-permute-start | bytes 1720328 | tf_op jit(solution)/shard_map/ppermute | solution.py:69
  85.9 116.8 %collective-permute-start.19 = (bf16[1280,1536]{1,0:T(8,128)(2,1)}, bf16[1280,1536]{1,0:T(8,128)(2,1)}, u32[]{:S(2)}, u32[]{:S(2)}) collective-permute-start(bf16[1280,1536]{1,0:T(8,128)(2,1)} %get-tuple-element.17), channel_id=1, source_target_pairs={{8,1},{1,8},{10,3},{3,10},{12,5},{5,12},{14,7},{7,14},{24,17},{17,... | collective-permute-start | bytes 11796488 | tf_op jit(solution)/shard_map/ppermute | solution.py:134
  87.9 8.4 %collective-permute-start.11 = (bf16[40,896]{1,0:T(8,128)(2,1)S(1)}, bf16[40,896]{1,0:T(8,128)(2,1)S(1)}, u32[]{:S(2)}, u32[]{:S(2)}) collective-permute-start(bf16[40,896]{1,0:T(8,128)(2,1)S(1)} %slice.303), channel_id=1, source_target_pairs={{0,4},{4,64},{64,68},{68,0},{1,5},{5,65},{65,69},{69,1},{2,6},{6,6... | collective-permute-start | bytes 215048 | tf_op jit(solution)/shard_map/ppermute | solution.py:70
  96.9 9.3 %collective-permute-start.6 = (bf16[160,896]{1,0:T(8,128)(2,1)S(1)}, bf16[160,896]{1,0:T(8,128)(2,1)S(1)}, u32[]{:S(2)}, u32[]{:S(2)}) collective-permute-start(bf16[160,896]{1,0:T(8,128)(2,1)S(1)} %slice.290), channel_id=1, source_target_pairs={{0,4},{4,64},{64,68},{68,0},{1,5},{5,65},{65,69},{69,1},{2,6},{6,6... | collective-permute-start | bytes 860168 | tf_op jit(solution)/shard_map/ppermute | solution.py:70
  100.5 20.4 %collective-permute-start.13 = (bf16[320,896]{1,0:T(8,128)(2,1)}, bf16[320,896]{1,0:T(8,128)(2,1)S(1)}, u32[]{:S(2)}, u32[]{:S(2)}) collective-permute-start(bf16[320,896]{1,0:T(8,128)(2,1)} %get-tuple-element.59), channel_id=1, source_target_pairs={{0,16},{16,32},{32,48},{48,0},{1,17},{17,33},{33,49},{49,1},{2,18}... | collective-permute-start | bytes 1720328 | tf_op jit(solution)/shard_map/ppermute | solution.py:68
  101.3 7.4 %collective-permute-start.7 = (bf16[160,896]{1,0:T(8,128)(2,1)S(1)}, bf16[160,896]{1,0:T(8,128)(2,1)S(1)}, u32[]{:S(2)}, u32[]{:S(2)}) collective-permute-start(bf16[160,896]{1,0:T(8,128)(2,1)S(1)} %slice.291), channel_id=1, source_target_pairs={{0,68},{4,0},{64,4},{68,64},{1,69},{5,1},{65,5},{69,65},{2,70},{6,... | collective-permute-start | bytes 860168 | tf_op jit(solution)/shard_map/ppermute | solution.py:71
  109.5 35.6 %collective-permute-start.8 = (bf16[1280,896]{1,0:T(8,128)(2,1)}, bf16[1280,896]{1,0:T(8,128)(2,1)}, u32[]{:S(2)}, u32[]{:S(2)}) collective-permute-start(bf16[1280,896]{1,0:T(8,128)(2,1)} %constant_dynamic-update-slice_fusion.5), channel_id=1, source_target_pairs={{0,8},{8,0},{1,9},{9,1},{2,10},{10,2},{3,11},{11,3},{4,12},{12,4},... | collective-permute-start | bytes 6881288 | tf_op jit(solution)/shard_map/ppermute | solution.py:144
  117.7 15.7 %collective-permute-start.14 = (bf16[320,896]{1,0:T(8,128)(2,1)}, bf16[320,896]{1,0:T(8,128)(2,1)S(1)}, u32[]{:S(2)}, u32[]{:S(2)}) collective-permute-start(bf16[320,896]{1,0:T(8,128)(2,1)} %get-tuple-element.59), channel_id=1, source_target_pairs={{0,48},{16,0},{32,16},{48,32},{1,49},{17,1},{33,17},{49,33},{2,50}... | collective-permute-start | bytes 1720328 | tf_op jit(solution)/shard_map/ppermute | solution.py:69
  121.0 17.6 %collective-permute-start.15 = (bf16[160,896]{1,0:T(8,128)(2,1)S(1)}, bf16[160,896]{1,0:T(8,128)(2,1)S(1)}, u32[]{:S(2)}, u32[]{:S(2)}) collective-permute-start(bf16[160,896]{1,0:T(8,128)(2,1)S(1)} %slice.305), channel_id=1, source_target_pairs={{0,16},{16,32},{32,48},{48,0},{1,17},{17,33},{33,49},{49,1},{2,18}... | collective-permute-start | bytes 860168 | tf_op jit(solution)/shard_map/ppermute | solution.py:70
  133.4 8.7 %collective-permute-start.16 = (bf16[160,896]{1,0:T(8,128)(2,1)S(1)}, bf16[160,896]{1,0:T(8,128)(2,1)S(1)}, u32[]{:S(2)}, u32[]{:S(2)}) collective-permute-start(bf16[160,896]{1,0:T(8,128)(2,1)S(1)} %slice.306), channel_id=1, source_target_pairs={{0,48},{16,0},{32,16},{48,32},{1,49},{17,1},{33,17},{49,33},{2,50}... | collective-permute-start | bytes 860168 | tf_op jit(solution)/shard_map/ppermute | solution.py:71
  142.9 12.4 %collective-permute-start.17 = (bf16[1280,896]{1,0:T(8,128)(2,1)}, bf16[1280,896]{1,0:T(8,128)(2,1)}, u32[]{:S(2)}, u32[]{:S(2)}) collective-permute-start(bf16[1280,896]{1,0:T(8,128)(2,1)} %constant_dynamic-update-slice_fusion.24), channel_id=1, source_target_pairs={{0,8},{8,0},{1,9},{9,1},{2,10},{10,2},{3,11},{11,3},{4,12},{12,4},... | collective-permute-start | bytes 6881288 | tf_op jit(solution)/shard_map/ppermute | solution.py:143
  177.8 19.4 %all-to-all-start.1 = ((bf16[8,128,512]{2,1,0:T(8,128)(2,1)}), bf16[8,128,512]{2,1,0:T(8,128)(2,1)S(1)}, u32[]{:S(2)}, u32[]{:S(2)}) async-start(bf16[8,128,512]{2,1,0:T(8,128)(2,1)} %broadcast_in_dim.60), calls=%async_computation.1 | async-start | bytes 2097152 | tf_op jit(solution)/shard_map/all_to_all | solution.py:59
  279.5 10.3 %collective-permute-start.21 = (bf16[1024,2560]{1,0:T(8,128)(2,1)}, bf16[1024,2560]{1,0:T(8,128)(2,1)}, u32[]{:S(2)}, u32[]{:S(2)}) collective-permute-start(bf16[1024,2560]{1,0:T(8,128)(2,1)} %bitcast.43), channel_id=1, source_target_pairs={{0,8},{8,0},{1,9},{9,1},{2,10},{10,2},{3,11},{11,3},{4,12},{12,4},... | collective-permute-start | bytes 15728648 | tf_op jit(solution)/shard_map/ppermute | solution.py:234
  281.1 47.3 %collective-permute-start.20 = (bf16[768,2560]{1,0:T(8,128)(2,1)}, bf16[768,2560]{1,0:T(8,128)(2,1)}, u32[]{:S(2)}, u32[]{:S(2)}) collective-permute-start(bf16[768,2560]{1,0:T(8,128)(2,1)} %bitcast.47), channel_id=1, source_target_pairs={{8,1},{1,8},{10,3},{3,10},{12,5},{5,12},{14,7},{7,14},{24,17},{17,... | collective-permute-start | bytes 11796488 | tf_op jit(solution)/shard_map/ppermute | solution.py:135
  336.4 23.8 %collective-permute-start.22 = (bf16[1024,2560]{1,0:T(8,128)(2,1)S(1)}, bf16[1024,2560]{1,0:T(8,128)(2,1)S(1)}, u32[]{:S(2)}, u32[]{:S(2)}) collective-permute-start(bf16[1024,2560]{1,0:T(8,128)(2,1)S(1)} %convolution_convert_fusion), channel_id=1, source_target_pairs={{0,8},{8,0},{1,9},{9,1},{2,10},{10,2},{3,11},{11,3},{4,12},{12,4},... | collective-permute-start | bytes 15728648 | tf_op jit(solution)/shard_map/ppermute | solution.py:238
  363.9 75.1 %all-to-all-start.4 = ((bf16[64,16,2560]{2,1,0:T(8,128)(2,1)}), bf16[64,16,2560]{2,1,0:T(8,128)(2,1)}, u32[]{:S(2)}, u32[]{:S(2)}) async-start(bf16[64,16,2560]{2,1,0:T(8,128)(2,1)} %bitcast.174), calls=%async_computation.4 | async-start | bytes 10485760 | tf_op jit(solution)/shard_map/all_to_all | solution.py:241
  444.2 15.0 %all-to-all-start.5 = ((bf16[8,16,2560]{2,1,0:T(8,128)(2,1)}), bf16[8,16,2560]{2,1,0:T(8,128)(2,1)S(1)}, u32[]{:S(2)}, u32[]{:S(2)}) async-start(bf16[8,16,2560]{2,1,0:T(8,128)(2,1)} %bitcast.51), calls=%async_computation.5 | async-start | bytes 1310720 | tf_op jit(solution)/shard_map/all_to_all | solution.py:250
  (11 other events, 181.4 us)
Sparse Core Ops, SparseCore 0:
  33.0 75.0 all-gather.1
